TPU v7x, 32 devices: a whole 2x2x4 slice. The times are simulated.
32 devices in a mesh: head: 2 (over y), blk: 16 (over z, x, core).
Axes of the slice: x: 2, y: 2, z: 4, core: 2. Of those that a mesh axis runs over, the one named last changes fastest.
Arguments:
- tokens: bfloat16 [4096, 1024], P(('blk', 'head')), may hold values from -6 to 6
- segments: int32 [4096], replicated, may hold values from 0 to 23, never falling along the last dimension, each value on 1 to 2560 neighbouring positions
- cotangent: bfloat16 [4096, 1024], P(('blk', 'head')), may hold values from -6 to 6
- w_query: bfloat16 [1024, 1024], P(('head', 'blk')), may hold values from -0.1875 to 0.1875
- w_key: bfloat16 [1024, 1024], P(('head', 'blk')), may hold values from -0.1875 to 0.1875
- w_value: bfloat16 [1024, 1024], P(('head', 'blk')), may hold values from -0.1875 to 0.1875
- b_query: bfloat16 [1024], P(('head', 'blk')), may hold values from -3 to 3
- b_value: bfloat16 [1024], P(('head', 'blk')), may hold values from -3 to 3
- w_output: bfloat16 [1024, 1024], P(('head', 'blk')), may hold values from -1.5 to 1.5
- b_output: bfloat16 [1024], P(('head', 'blk')), may hold values from -3 to 3
- gain_attn: bfloat16 [1024], P(('head', 'blk')), may hold values from 0.5 to 1.5
- shift_attn: bfloat16 [1024], P(('head', 'blk')), may hold values from -2 to 2
- w_inner: bfloat16 [1024, 4096], P(('head', 'blk')), may hold values from -0.1875 to 0.1875
- b_inner: bfloat16 [4096], P(('head', 'blk')), may hold values from -3 to 3
- w_outer: bfloat16 [4096, 1024], P(('head', 'blk')), may hold values from -0.09375 to 0.09375
- b_outer: bfloat16 [1024], P(('head', 'blk')), may hold values from -3 to 3
- gain_ffn: bfloat16 [1024], P(('head', 'blk')), may hold values from 0.5 to 1.5
- shift_ffn: bfloat16 [1024], P(('head', 'blk')), may hold values from -2 to 2
Outputs:
- out_rows: bfloat16 [4096, 1024], P(('blk', 'head'))
- grad_tokens: float32 [4096, 1024], P(('blk', 'head'))
- grad_wq: float32 [1024, 1024], P(('head', 'blk'))
- grad_wk: float32 [1024, 1024], P(('head', 'blk'))
- grad_wv: float32 [1024, 1024], P(('head', 'blk'))
- grad_bq: float32 [1024], P(('head', 'blk'))
- grad_bv: float32 [1024], P(('head', 'blk'))
- grad_wo: float32 [1024, 1024], P(('head', 'blk'))
- grad_bo: float32 [1024], P(('head', 'blk'))
- grad_g1: float32 [1024], P(('head', 'blk'))
- grad_n1: float32 [1024], P(('head', 'blk'))
- grad_w1: float32 [1024, 4096], P(('head', 'blk'))
- grad_b1: float32 [4096], P(('head', 'blk'))
- grad_w2: float32 [4096, 1024], P(('head', 'blk'))
- grad_b2: float32 [1024], P(('head', 'blk'))
- grad_g2: float32 [1024], P(('head', 'blk'))
- grad_n2: float32 [1024], P(('head', 'blk'))
Inputs may be any that keep to these rules, and one draw needn't show every extreme that they name: `segments`: segment numbers never fall along the stream; each document holds 1 to 2560 tokens, and one holds exactly 2560.
All inputs are finite; a program needn't handle non-finite values.
Results may differ from a plain program's by a relative error of at most 0.019.
Values may be sent and summed in bfloat16 or wider, within the bound.
No kernel may reach another device: no remote copies, remote signals or barrier semaphores. Data moves between devices by JAX's collectives and lax.ppermute only.
A program may use at most 192 MiB of HBM per device.

v0:
```python
import math
import jax
import jax.numpy as jnp
from jax import lax
from jax.sharding import PartitionSpec as P

H = 16
HD = 64
EPS = 1e-05
NEG = -1e30


def passed_along(value, axis, steps):
    count = lax.axis_size(axis)
    pairs = [(source, (source + steps) % count) for source in range(count)]
    return lax.ppermute(value, axis, pairs)


def layer_norm(hidden, gain_row, shift_row):
    centre = hidden - jnp.mean(hidden, axis=-1, keepdims=True)
    spread = jnp.mean(centre * centre, axis=-1, keepdims=True)
    return centre * lax.rsqrt(spread + EPS) * gain_row + shift_row


def exact_gelu(values):
    return jax.nn.gelu(values, approximate=False)


def row_sum(matrix):
    return jnp.sum(matrix.astype(jnp.float32), axis=0)


def left_product(former, latter):
    return lax.dot_general(
        former, latter, (((0,), (0,)), ((), ())), preferred_element_type=jnp.float32
    )


def right_product(former, latter):
    return lax.dot_general(
        former, latter, (((1,), (1,)), ((), ())), preferred_element_type=jnp.float32
    )


def intersections(query_segs, key_segs):
    return jnp.logical_and(key_segs[0] <= query_segs[-1], query_segs[0] <= key_segs[-1])


def fold_block(running, block_item, query_heads, query_segs, score_scale):
    key_block, value_block, key_segs = block_item
    running_max, weight_sum, mixed = running
    scores = (
        jnp.einsum("qgd,kgd->gqk", query_heads, key_block, preferred_element_type=jnp.float32)
        * score_scale
    )
    same = query_segs[:, None] == key_segs[None, :]
    scores = jnp.where(same[None], scores, NEG)
    new_max = jnp.maximum(running_max, jnp.max(scores, axis=-1))
    factor = jnp.exp(running_max - new_max)
    expo = jnp.exp(scores - new_max[:, :, None])
    weight_sum = weight_sum * factor + jnp.sum(expo, axis=-1)
    mixed = mixed * factor[:, :, None] + jnp.einsum(
        "gqk,kgd->gqd", expo.astype(jnp.bfloat16), value_block, preferred_element_type=jnp.float32
    )
    return (new_max, weight_sum, mixed)


def pair_terms(
    query_blk, grad_blk, log_blk, delta_blk, query_segs, key_blk, value_blk, key_segs, score_scale
):
    scores = (
        jnp.einsum("qgd,kgd->gqk", query_blk, key_blk, preferred_element_type=jnp.float32)
        * score_scale
    )
    same = query_segs[:, None] == key_segs[None, :]
    scores = jnp.where(same[None], scores, NEG)
    prob = jnp.exp(scores - log_blk[:, :, None])
    grad_prob = jnp.einsum("qgd,kgd->gqk", grad_blk, value_blk, preferred_element_type=jnp.float32)
    grad_score = (prob * (grad_prob - delta_blk[:, :, None])).astype(jnp.bfloat16)
    value_term = jnp.einsum(
        "gqk,qgd->kgd", prob.astype(jnp.bfloat16), grad_blk, preferred_element_type=jnp.float32
    )
    key_term = (
        jnp.einsum("gqk,qgd->kgd", grad_score, query_blk, preferred_element_type=jnp.float32)
        * score_scale
    )
    query_term = (
        jnp.einsum("gqk,kgd->qgd", grad_score, key_blk, preferred_element_type=jnp.float32)
        * score_scale
    )
    return (key_term, value_term, query_term)


def body(
    tokens,
    segments,
    cotangent,
    w_query,
    w_key,
    w_value,
    b_query,
    b_value,
    w_output,
    b_output,
    gain_attn,
    shift_attn,
    w_inner,
    b_inner,
    w_outer,
    b_outer,
    gain_ffn,
    shift_ffn,
):
    gathered = (
        lax.all_gather(w_query, ("head", "blk"), axis=0, tiled=True),
        lax.all_gather(w_key, ("head", "blk"), axis=0, tiled=True),
        lax.all_gather(w_value, ("head", "blk"), axis=0, tiled=True),
        lax.all_gather(b_query, ("head", "blk"), axis=0, tiled=True),
        lax.all_gather(b_value, ("head", "blk"), axis=0, tiled=True),
        lax.all_gather(w_output, ("head", "blk"), axis=0, tiled=True),
        lax.all_gather(b_output, ("head", "blk"), axis=0, tiled=True),
        lax.all_gather(gain_attn, ("head", "blk"), axis=0, tiled=True),
        lax.all_gather(shift_attn, ("head", "blk"), axis=0, tiled=True),
        lax.all_gather(w_inner, ("head", "blk"), axis=0, tiled=True),
        lax.all_gather(b_inner, ("head", "blk"), axis=0, tiled=True),
        lax.all_gather(w_outer, ("head", "blk"), axis=0, tiled=True),
        lax.all_gather(b_outer, ("head", "blk"), axis=0, tiled=True),
        lax.all_gather(gain_ffn, ("head", "blk"), axis=0, tiled=True),
        lax.all_gather(shift_ffn, ("head", "blk"), axis=0, tiled=True),
    )
    (
        full_wq,
        full_wk,
        full_wv,
        full_bq,
        full_bv,
        full_wo,
        full_bo,
        full_g1,
        full_n1,
        full_w1,
        full_b1,
        full_w2,
        full_b2,
        full_g2,
        full_n2,
    ) = gathered
    head_count = lax.axis_size("head")
    cycle_size = lax.axis_size("blk")
    head_group = H // head_count
    head_width = head_group * HD
    score_scale = HD ** (-0.5)
    inputs = tokens.astype(jnp.float32)
    query_tok = (
        jnp.dot(tokens, full_wq, preferred_element_type=jnp.float32) + full_bq.astype(jnp.float32)
    ).astype(jnp.bfloat16)
    key_tok = jnp.dot(tokens, full_wk, preferred_element_type=jnp.float32).astype(jnp.bfloat16)
    value_tok = (
        jnp.dot(tokens, full_wv, preferred_element_type=jnp.float32) + full_bv.astype(jnp.float32)
    ).astype(jnp.bfloat16)
    query_cols, key_cols, value_cols = (
        lax.all_to_all(query_tok, "head", split_axis=1, concat_axis=0, tiled=True),
        lax.all_to_all(key_tok, "head", split_axis=1, concat_axis=0, tiled=True),
        lax.all_to_all(value_tok, "head", split_axis=1, concat_axis=0, tiled=True),
    )
    row_count = query_cols.shape[0]
    cycle_index = lax.axis_index("blk")
    query_segs = lax.dynamic_slice_in_dim(segments, cycle_index * row_count, row_count)
    query_heads = query_cols.reshape(row_count, head_group, HD)
    initial = (
        jnp.full((head_group, row_count), NEG, jnp.float32),
        jnp.zeros((head_group, row_count), jnp.float32),
        jnp.zeros((head_group, row_count, HD), jnp.float32),
    )
    running = initial
    key_piece = lax.all_gather(key_cols, "blk", axis=0, tiled=True)
    value_piece = lax.all_gather(value_cols, "blk", axis=0, tiled=True)
    piece_rows = key_piece.shape[0]
    block_rows = math.gcd(piece_rows, 1024)
    block_count = piece_rows // block_rows
    key_segs = segments
    stacked = (
        key_piece.reshape(block_count, block_rows, head_group, HD),
        value_piece.reshape(block_count, block_rows, head_group, HD),
        key_segs.reshape(block_count, block_rows),
    )

    def visit(current, block_item):

        def update(inner_state):
            return fold_block(inner_state, block_item, query_heads, query_segs, score_scale)

        def visit_unchanged(inner_state):
            return inner_state

        current = lax.cond(
            intersections(query_segs, block_item[2]), update, visit_unchanged, current
        )
        return (current, None)

    running, _ = lax.scan(visit, running, stacked)
    running_max, weight_sum, mixed = running
    log_sum = running_max + jnp.log(weight_sum)
    context = jnp.transpose(mixed / weight_sum[:, :, None], (1, 0, 2))
    context_cols = context.astype(jnp.bfloat16).reshape(row_count, head_width)
    context_tok = lax.all_to_all(context_cols, "head", split_axis=0, concat_axis=1, tiled=True)
    attn_out = jnp.dot(context_tok, full_wo, preferred_element_type=jnp.float32) + full_bo.astype(
        jnp.float32
    )
    resid_one = inputs + attn_out
    norm_one = layer_norm(resid_one, full_g1.astype(jnp.float32), full_n1.astype(jnp.float32))
    inner_in = norm_one.astype(jnp.bfloat16)
    pre_act = jnp.dot(inner_in, full_w1, preferred_element_type=jnp.float32) + full_b1.astype(
        jnp.float32
    )
    activation = exact_gelu(pre_act).astype(jnp.bfloat16)
    outer_out = jnp.dot(activation, full_w2, preferred_element_type=jnp.float32) + full_b2.astype(
        jnp.float32
    )
    resid_two = norm_one + outer_out
    out_rows = layer_norm(
        resid_two, full_g2.astype(jnp.float32), full_n2.astype(jnp.float32)
    ).astype(jnp.bfloat16)
    back_wq, back_wk, back_wv, back_wo, back_w1, back_w2, back_g1, back_g2 = (
        lax.all_gather(w_query, ("head", "blk"), axis=0, tiled=True),
        lax.all_gather(w_key, ("head", "blk"), axis=0, tiled=True),
        lax.all_gather(w_value, ("head", "blk"), axis=0, tiled=True),
        lax.all_gather(w_output, ("head", "blk"), axis=0, tiled=True),
        lax.all_gather(w_inner, ("head", "blk"), axis=0, tiled=True),
        lax.all_gather(w_outer, ("head", "blk"), axis=0, tiled=True),
        lax.all_gather(gain_attn, ("head", "blk"), axis=0, tiled=True),
        lax.all_gather(gain_ffn, ("head", "blk"), axis=0, tiled=True),
    )
    _, back_two = jax.vjp(
        layer_norm, resid_two, back_g2.astype(jnp.float32), full_n2.astype(jnp.float32)
    )
    grad_resid_two, grad_g2, grad_n2 = back_two(cotangent.astype(jnp.float32))
    grad_outer = grad_resid_two.astype(jnp.bfloat16)
    grad_b2 = row_sum(grad_outer)
    grad_w2 = left_product(activation, grad_outer)
    grad_act = right_product(grad_outer, back_w2)
    _, gelu_back = jax.vjp(exact_gelu, pre_act)
    grad_pre = gelu_back(grad_act)[0].astype(jnp.bfloat16)
    grad_b1 = row_sum(grad_pre)
    grad_w1 = left_product(inner_in, grad_pre)
    grad_norm_one = grad_resid_two + right_product(grad_pre, back_w1)
    _, back_one = jax.vjp(
        layer_norm, resid_one, back_g1.astype(jnp.float32), full_n1.astype(jnp.float32)
    )
    grad_resid_one, grad_g1, grad_n1 = back_one(grad_norm_one)
    grad_attn = grad_resid_one.astype(jnp.bfloat16)
    grad_bo = row_sum(grad_attn)
    grad_wo = left_product(context_tok, grad_attn)
    grad_context = right_product(grad_attn, back_wo).astype(jnp.bfloat16)
    grad_cols = lax.all_to_all(grad_context, "head", split_axis=1, concat_axis=0, tiled=True)
    grad_heads = grad_cols.reshape(row_count, head_group, HD)
    delta_rows = jnp.transpose(jnp.sum(grad_heads.astype(jnp.float32) * context, axis=-1))
    key_heads = key_cols.reshape(row_count, head_group, HD)
    value_heads = value_cols.reshape(row_count, head_group, HD)
    zero_grad = jnp.zeros((row_count, head_group, HD), jnp.float32)

    def cycle_turn(turn_index, cycle_state):
        key_now, value_now, key_grad, value_grad, query_grad = cycle_state
        source = jnp.mod(cycle_index - turn_index, cycle_size)
        key_segs = lax.dynamic_slice_in_dim(segments, source * row_count, row_count)

        def pair_grads(grad_parts):
            part_key, part_value, part_query = grad_parts
            key_term, value_term, query_term = pair_terms(
                query_heads,
                grad_heads,
                log_sum,
                delta_rows,
                query_segs,
                key_now,
                value_now,
                key_segs,
                score_scale,
            )
            return (part_key + key_term, part_value + value_term, part_query + query_term)

        def cycle_unchanged(grad_parts):
            return grad_parts

        key_grad, value_grad, query_grad = lax.cond(
            intersections(query_segs, key_segs),
            pair_grads,
            cycle_unchanged,
            (key_grad, value_grad, query_grad),
        )
        key_now, value_now = passed_along((key_now, value_now), "blk", 1)
        key_grad, value_grad = (
            passed_along(key_grad.astype(jnp.bfloat16), "blk", 1).astype(key_grad.dtype),
            passed_along(value_grad.astype(jnp.bfloat16), "blk", 1).astype(value_grad.dtype),
        )
        return (key_now, value_now, key_grad, value_grad, query_grad)

    final_state = lax.fori_loop(
        0, cycle_size, cycle_turn, (key_heads, value_heads, zero_grad, zero_grad, zero_grad)
    )
    grad_key_heads = final_state[2]
    grad_value_heads = final_state[3]
    grad_query_heads = final_state[4]
    grad_query_tok, grad_key_tok, grad_value_tok = (
        lax.all_to_all(
            grad_query_heads.astype(jnp.bfloat16).reshape(row_count, head_width),
            "head",
            split_axis=0,
            concat_axis=1,
            tiled=True,
        ),
        lax.all_to_all(
            grad_key_heads.astype(jnp.bfloat16).reshape(row_count, head_width),
            "head",
            split_axis=0,
            concat_axis=1,
            tiled=True,
        ),
        lax.all_to_all(
            grad_value_heads.astype(jnp.bfloat16).reshape(row_count, head_width),
            "head",
            split_axis=0,
            concat_axis=1,
            tiled=True,
        ),
    )
    grad_bq = row_sum(grad_query_tok)
    grad_bv = row_sum(grad_value_tok)
    grad_wq = left_product(tokens, grad_query_tok)
    grad_wk = left_product(tokens, grad_key_tok)
    grad_wv = left_product(tokens, grad_value_tok)
    grad_tokens = (
        grad_resid_one
        + right_product(grad_query_tok, back_wq)
        + right_product(grad_key_tok, back_wk)
        + right_product(grad_value_tok, back_wv)
    )
    shards = (
        lax.psum_scatter(grad_wq, ("head", "blk"), scatter_dimension=0, tiled=True),
        lax.psum_scatter(grad_wk, ("head", "blk"), scatter_dimension=0, tiled=True),
        lax.psum_scatter(grad_wv, ("head", "blk"), scatter_dimension=0, tiled=True),
        lax.psum_scatter(grad_bq, ("head", "blk"), scatter_dimension=0, tiled=True),
        lax.psum_scatter(grad_bv, ("head", "blk"), scatter_dimension=0, tiled=True),
        lax.psum_scatter(grad_wo, ("head", "blk"), scatter_dimension=0, tiled=True),
        lax.psum_scatter(grad_bo, ("head", "blk"), scatter_dimension=0, tiled=True),
        lax.psum_scatter(grad_g1, ("head", "blk"), scatter_dimension=0, tiled=True),
        lax.psum_scatter(grad_n1, ("head", "blk"), scatter_dimension=0, tiled=True),
        lax.psum_scatter(grad_w1, ("head", "blk"), scatter_dimension=0, tiled=True),
        lax.psum_scatter(grad_b1, ("head", "blk"), scatter_dimension=0, tiled=True),
        lax.psum_scatter(grad_w2, ("head", "blk"), scatter_dimension=0, tiled=True),
        lax.psum_scatter(grad_b2, ("head", "blk"), scatter_dimension=0, tiled=True),
        lax.psum_scatter(grad_g2, ("head", "blk"), scatter_dimension=0, tiled=True),
        lax.psum_scatter(grad_n2, ("head", "blk"), scatter_dimension=0, tiled=True),
    )
    return (out_rows, grad_tokens) + tuple(shards)


def solution(mesh):
    placed = (
        P(("blk", "head"), None),
        P(),
        P(("blk", "head"), None),
        P(("head", "blk"), None),
        P(("head", "blk"), None),
        P(("head", "blk"), None),
        P(("head", "blk")),
        P(("head", "blk")),
        P(("head", "blk"), None),
        P(("head", "blk")),
        P(("head", "blk")),
        P(("head", "blk")),
        P(("head", "blk"), None),
        P(("head", "blk")),
        P(("head", "blk"), None),
        P(("head", "blk")),
        P(("head", "blk")),
        P(("head", "blk")),
    )
    return jax.shard_map(
        body,
        mesh=mesh,
        in_specs=placed,
        out_specs=(
            P(("blk", "head"), None),
            P(("blk", "head"), None),
            P(("head", "blk"), None),
            P(("head", "blk"), None),
            P(("head", "blk"), None),
            P(("head", "blk")),
            P(("head", "blk")),
            P(("head", "blk"), None),
            P(("head", "blk")),
            P(("head", "blk")),
            P(("head", "blk")),
            P(("head", "blk"), None),
            P(("head", "blk")),
            P(("head", "blk"), None),
            P(("head", "blk")),
            P(("head", "blk")),
            P(("head", "blk")),
        ),
        check_vma=False,
    )
```

profile of v0, /device:TPU:4, one launch (start us, length us, event | category | flops | bytes accessed | tf_op | source)
XLA Modules:
  0.0 1730.0 jit_solution(9327280273881781329)
XLA Ops:
  9.5 59.1 %all-gather.10.cloned.1.call-done = bf16[1024,1024]{1,0:T(8,128)(2,1)} async-done(((bf16[32,1024]{1,0:T(8,128)(2,1)}), bf16[1024,1024]{1,0:T(8,128)(2,1)}) %all-gather.10.cloned.1.call-update) | async-done | bytes 2097168 | tf_op jit(solution)/shard_map/all_gather | solution.py:116
  70.8 7.8 all_to_all.146
  80.6 40.7 %all-reduce.18 = (bf16[1024]{0:T(1024)(128)(2,1)S(1)}, bf16[1024]{0:T(1024)(128)(2,1)S(1)}, bf16[1024]{0:T(1024)(128)(2,1)S(1)}, bf16[1024]{0:T(1024)(128)(2,1)S...) all-reduce(bf16[1024]{0:T(1024)(128)(2,1)S(1)} %dynamic-update-slic, ...), channel_id=1, replica_groups=mesh['head'=2,'blk'=16] {'head','blk'}, use_global_device_ids=true, to_apply=%add | all-reduce | flops 8192 | bytes 32768
  121.3 5.9 all-gather.16.cloned.1.call-done
  129.2 7.8 all_to_all.147
  139.2 46.2 %all-gather.14.cloned.1.call-done = bf16[1024,1024]{1,0:T(8,128)(2,1)} async-done(((bf16[32,1024]{1,0:T(8,128)(2,1)}), bf16[1024,1024]{1,0:T(8,128)(2,1)}) %all-gather.14.cloned.1.call-update) | async-done | bytes 2097168 | tf_op jit(solution)/shard_map/all_gather | solution.py:115
  188.1 4.0 all-to-all-start.1
  192.1 39.4 %all-gather = bf16[32,1,128]{2,1,0:T(2,128)(2,1)S(1)} all-gather(bf16[1,1,128]{2,1,0:T(2,128)(2,1)S(1)} %bitcast.197), channel_id=1, replica_groups=mesh['head'=2,'blk'=16] {'head','blk'}, dimensions={0}, use_global_device_ids=true | all-gather | bytes 8448 | tf_op jit(solution)/shard_map/all_gather | solution.py:125
  233.4 3.7 all-gather.12.cloned.1.call-done
  237.0 11.3 reshape.263
  248.3 9.9 copy.106
  258.2 30.1 %all-gather.18.cloned.1.call-done = bf16[4096,512]{1,0:T(8,128)(2,1)} async-done(((bf16[256,512]{1,0:T(8,128)(2,1)}), bf16[4096,512]{1,0:T(8,128)(2,1)}) %all-gather.18.cloned.1.call-update) | async-done | bytes 4194320 | tf_op jit(solution)/shard_map/all_gather | solution.py:177
  288.3 11.2 reshape.264
  299.5 9.8 copy.107
  309.3 23.4 %while.38 = (s32[]{:T(128)}, f32[8,256]{1,0:T(8,128)S(1)}, f32[8,256]{1,0:T(8,128)S(1)}, f32[8,256,64]{1,2,0:T(8,128)S(1)}, s32[4,1024]{1,0:T(4,128)S(1)}, /*ind...) while((s32[]{:T(128)}, f32[8,256]{1,0:T(8,128)S(1)}, ...), condition=%wide.region_5.6_spmd, body=%wide.region_0.5_spmd.sunk | while | flops 560467968 | bytes 29768016 | solution.py:201
  313.1 8.1 conditional.5
  317.9 3.3 fusion.6
  333.7 4.1 all-to-all-start.3
  337.8 8.2 all-gather.20.cloned.1.call-done
  348.4 76.9 %all-gather.22.cloned.1.call-done = bf16[1024,4096]{1,0:T(8,128)(2,1)} async-done(((bf16[32,4096]{1,0:T(8,128)(2,1)}), bf16[1024,4096]{1,0:T(8,128)(2,1)}) %all-gather.22.cloned.1.call-update) | async-done | bytes 8388624 | tf_op jit(solution)/shard_map/all_gather | solution.py:124
  425.3 9.7 multiply_convert_fusion.1
  435.0 69.3 %all-gather.24.cloned.1.call-done = bf16[4096,1024]{1,0:T(8,128)(2,1)} async-done(((bf16[128,1024]{1,0:T(8,128)(2,1)}), bf16[4096,1024]{1,0:T(8,128)(2,1)}) %all-gather.24.cloned.1.call-update) | async-done | bytes 8388624 | tf_op jit(solution)/shard_map/all_gather | solution.py:126
  504.2 5.3 fusion.53
  511.3 5.3 convert_reduce_fusion
  516.7 3.1 multiply_reduce_fusion
  523.1 4.0 all-to-all-start.4
  531.7 384.5 %while.39 = (s32[]{:T(128)}, bf16[256,8,64]{0,2,1:T(8,128)(2,1)}, bf16[256,8,64]{0,2,1:T(8,128)(2,1)S(1)}, f32[256,8,64]{0,2,1:T(8,128)S(1)}, f32[256,8,64]{0,2,...) while((s32[]{:T(128)}, bf16[256,8,64]{0,2,1:T(8,128)(2,1)}, ...), condition=%wide.region_18.19_spmd.clone, body=%wide.region_15.18_spmd.clone.sunk | while | flops 340721696 | bytes 25055948 | solution.py:298
  542.8 5.2 collective-permute-done.2
  548.0 3.7 collective-permute-done.3
  568.9 4.2 collective-permute-done.2
  592.1 5.6 collective-permute-done.2
  597.7 3.6 collective-permute-done.3
  615.0 8.1 collective-permute-done.2
  623.1 3.6 collective-permute-done.3
  639.6 8.9 collective-permute-done.2
  648.5 3.6 collective-permute-done.3
  655.1 3.2 collective-permute-done.1
  664.7 8.9 collective-permute-done.2
  673.6 3.5 collective-permute-done.3
  680.1 3.2 collective-permute-done.1
  689.7 8.2 collective-permute-done.2
  712.7 8.2 collective-permute-done.2
  735.8 8.2 collective-permute-done.2
  758.8 8.2 collective-permute-done.2
  781.8 8.2 collective-permute-done.2
  804.8 8.2 collective-permute-done.2
  828.6 7.5 collective-permute-done.2
  852.5 6.6 collective-permute-done.2
  876.4 5.7 collective-permute-done.2
  900.2 7.5 collective-permute-done.2
  916.4 6.2 all_to_all.148
  926.0 5.4 copy.128
  931.6 7.6 all_to_all.149
  942.5 5.4 copy.130
  949.1 8.1 all_to_all.150
  959.9 5.4 copy.132
  966.6 8.2 fusion.42
  976.1 8.1 fusion.55
  985.5 40.6 %all-reduce.17 = (f32[1024]{0:T(1024)S(1)}, f32[1024]{0:T(1024)S(1)}, f32[1024]{0:T(1024)S(1)}, f32[1024]{0:T(1024)S(1)}, f32[1024]{0:T(1024)S(1)}, /*index=5*/f...) all-reduce(f32[1024]{0:T(1024)S(1)} %bitcast.194, ...), channel_id=5, replica_groups=mesh['head'=2,'blk'=16] {'head','blk'}, use_global_device_ids=true, to_apply=%region_23.24.clone | all-reduce | flops 12288 | bytes 98304
  1035.5 34.0 %reduce-scatter.19.cloned.1.call-done = f32[32,1024]{1,0:T(8,128)} async-done(((f32[1024,1024]{1,0:T(8,128)}), f32[32,1024]{1,0:T(8,128)}) %reduce-scatter.19.cloned.1.call-update) | async-done | bytes 131088
  1069.6 140.6 %reduce-scatter.21.cloned.1.call-done = f32[32,1024]{1,0:T(8,128)} async-done(((f32[1024,1024]{1,0:T(8,128)}), f32[32,1024]{1,0:T(8,128)}) %reduce-scatter.21.cloned.1.call-update) | async-done | bytes 131088
  1210.2 140.4 %reduce-scatter.23.cloned.1.call-done = f32[32,1024]{1,0:T(8,128)} async-done(((f32[1024,1024]{1,0:T(8,128)}), f32[32,1024]{1,0:T(8,128)}) %reduce-scatter.23.cloned.1.call-update) | async-done | bytes 131088
  1350.6 185.6 %reduce-scatter.15.cloned.1.call-done = f32[32,4096]{1,0:T(8,128)} async-done(((f32[1024,4096]{1,0:T(8,128)}), f32[32,4096]{1,0:T(8,128)}) %reduce-scatter.15.cloned.1.call-update) | async-done | bytes 524304 | tf_op jit(solution)/shard_map/reduce_scatter | solution.py:348
  1536.3 186.9 %reduce-scatter.17.cloned.1.call-done = f32[128,1024]{1,0:T(8,128)} async-done(((f32[4096,1024]{1,0:T(8,128)}), f32[128,1024]{1,0:T(8,128)}) %reduce-scatter.17.cloned.1.call-update) | async-done | bytes 524304 | tf_op jit(solution)/shard_map/reduce_scatter | solution.py:350
  (525 shorter events, 265.9 us)
Async XLA Ops:
  7.3 61.4 %all-gather.10.cloned.1.call-start = ((), (), s32[]{:S(2)}) async-start(), calls=%async_computation.14 | async-start | bytes 2162688 | tf_op jit(solution)/shard_map/all_gather | solution.py:116
  8.0 119.1 %all-gather.16.cloned.1.call-start = ((), (), s32[]{:S(2)}) async-start(), calls=%async_computation.17 | async-start | bytes 2162688 | tf_op jit(solution)/shard_map/all_gather | solution.py:117
  8.8 176.6 %all-gather.14.cloned.1.call-start = ((), (), s32[]{:S(2)}) async-start(), calls=%async_computation.16 | async-start | bytes 2162688 | tf_op jit(solution)/shard_map/all_gather | solution.py:115
  9.5 227.5 %all-gather.12.cloned.1.call-start = ((), (), s32[]{:S(2)}) async-start(), calls=%async_computation.15 | async-start | bytes 4456448 | tf_op jit(solution)/shard_map/all_gather | solution.py:176
  78.6 209.7 %all-gather.18.cloned.1.call-start = ((), (), s32[]{:S(2)}) async-start(), calls=%async_computation.18 | async-start | bytes 4456448 | tf_op jit(solution)/shard_map/all_gather | solution.py:177
  137.0 208.9 %all-gather.20.cloned.1.call-start = ((), (), s32[]{:S(2)}) async-start(), calls=%async_computation.19 | async-start | bytes 2162688 | tf_op jit(solution)/shard_map/all_gather | solution.py:120
  137.6 287.7 %all-gather.22.cloned.1.call-start = ((), (), s32[]{:S(2)}) async-start(), calls=%async_computation.20 | async-start | bytes 8650752 | tf_op jit(solution)/shard_map/all_gather | solution.py:124
  138.4 365.8 %all-gather.24.cloned.1.call-start = ((), (), s32[]{:S(2)}) async-start(), calls=%async_computation.21 | async-start | bytes 8650752 | tf_op jit(solution)/shard_map/all_gather | solution.py:126
  188.1 43.5 %all-to-all-start.1 = ((bf16[128,2,512]{2,0,1:T(8,128)(2,1)}), bf16[128,2,512]{2,0,1:T(8,128)(2,1)S(1)}, u32[]{:S(2)}, u32[]{:S(2)}) async-start(bf16[128,2,512]{2,0,1:T(8,128)(2,1)} %bitcast.154), calls=%async_computation.1 | async-start | bytes 524288 | tf_op jit(solution)/shard_map/all_to_all | solution.py:162
  333.7 12.3 all-to-all-start.3
  527.1 508.4 %reduce-scatter.13.cloned.1.call-start = ((), (), s32[]{:S(2)}) async-start(), calls=%async_computation.22 | async-start | bytes 4325376 | tf_op jit(solution)/shard_map/reduce_scatter | solution.py:344
  530.1 539.5 %reduce-scatter.19.cloned.1.call-start = ((), (), s32[]{:S(2)}) async-start(), calls=%async_computation.25 | async-start | bytes 4325376
  539.6 12.2 collective-permute-start.3
  541.1 13.9 collective-permute-start
  541.2 16.6 collective-permute-start.1
  564.5 11.6 collective-permute-start.3
  567.1 12.5 collective-permute-start
  567.1 15.5 collective-permute-start.1
  588.8 12.6 collective-permute-start.3
  589.8 15.0 collective-permute-start
  589.9 18.0 %collective-permute-start.1 = (bf16[256,8,64]{0,2,1:T(8,128)(2,1)S(1)}, bf16[256,8,64]{0,2,1:T(8,128)(2,1)S(1)}, u32[]{:S(2)}, u32[]{:S(2)}) collective-permute-start(bf16[256,8,64]{0,2,1:T(8,128)(2,1)S(1)} %copy.190), channel_id=1, source_target_pairs={{0,1},{1,2},{2,3},{3,4},{4,5},{5,6},{6,7},{7,8},{8,9},{9,10},{10,1... | collective-permute-start | bytes 786440 | tf_op jit(solution)/shard_map/while/body/eval_jaxpr/ppermute | solution.py:16
  614.0 12.8 collective-permute-start.3
  614.1 16.1 collective-permute-start
  614.2 19.1 %collective-permute-start.1 = (bf16[256,8,64]{0,2,1:T(8,128)(2,1)S(1)}, bf16[256,8,64]{0,2,1:T(8,128)(2,1)S(1)}, u32[]{:S(2)}, u32[]{:S(2)}) collective-permute-start(bf16[256,8,64]{0,2,1:T(8,128)(2,1)S(1)} %copy.190), channel_id=1, source_target_pairs={{0,1},{1,2},{2,3},{3,4},{4,5},{5,6},{6,7},{7,8},{8,9},{9,10},{10,1... | collective-permute-start | bytes 786440 | tf_op jit(solution)/shard_map/while/body/eval_jaxpr/ppermute | solution.py:16
  639.4 12.8 collective-permute-start.3
  639.5 15.6 collective-permute-start
  639.6 18.8 %collective-permute-start.1 = (bf16[256,8,64]{0,2,1:T(8,128)(2,1)S(1)}, bf16[256,8,64]{0,2,1:T(8,128)(2,1)S(1)}, u32[]{:S(2)}, u32[]{:S(2)}) collective-permute-start(bf16[256,8,64]{0,2,1:T(8,128)(2,1)S(1)} %copy.190), channel_id=1, source_target_pairs={{0,1},{1,2},{2,3},{3,4},{4,5},{5,6},{6,7},{7,8},{8,9},{9,10},{10,1... | collective-permute-start | bytes 786440 | tf_op jit(solution)/shard_map/while/body/eval_jaxpr/ppermute | solution.py:16
  664.5 12.6 collective-permute-start.3
  664.5 15.6 collective-permute-start
  664.6 18.8 %collective-permute-start.1 = (bf16[256,8,64]{0,2,1:T(8,128)(2,1)S(1)}, bf16[256,8,64]{0,2,1:T(8,128)(2,1)S(1)}, u32[]{:S(2)}, u32[]{:S(2)}) collective-permute-start(bf16[256,8,64]{0,2,1:T(8,128)(2,1)S(1)} %copy.190), channel_id=1, source_target_pairs={{0,1},{1,2},{2,3},{3,4},{4,5},{5,6},{6,7},{7,8},{8,9},{9,10},{10,1... | collective-permute-start | bytes 786440 | tf_op jit(solution)/shard_map/while/body/eval_jaxpr/ppermute | solution.py:16
  689.5 11.3 collective-permute-start.3
  689.6 14.1 collective-permute-start
  689.7 16.7 collective-permute-start.1
  712.5 11.3 collective-permute-start.3
  712.6 14.1 collective-permute-start
  712.7 16.7 collective-permute-start.1
  735.6 11.3 collective-permute-start.3
  735.6 14.1 collective-permute-start
  735.7 16.7 collective-permute-start.1
  758.6 11.3 collective-permute-start.3
  758.6 14.1 collective-permute-start
  758.7 16.7 collective-permute-start.1
  781.6 11.3 collective-permute-start.3
  781.7 14.1 collective-permute-start
  781.7 16.7 collective-permute-start.1
  804.6 11.3 collective-permute-start.3
  804.7 14.1 collective-permute-start
  804.7 16.7 collective-permute-start.1
  827.6 11.3 collective-permute-start.3
  827.7 14.1 collective-permute-start
  827.8 16.7 collective-permute-start.1
  850.6 11.3 collective-permute-start.3
  850.7 14.1 collective-permute-start
  850.8 16.7 collective-permute-start.1
  873.7 11.3 collective-permute-start.3
  873.7 14.1 collective-permute-start
  873.8 16.7 collective-permute-start.1
  899.3 11.3 collective-permute-start.3
  899.4 14.1 collective-permute-start
  899.5 16.7 collective-permute-start.1
  931.4 278.8 %reduce-scatter.21.cloned.1.call-start = ((), (), s32[]{:S(2)}) async-start(), calls=%async_computation.26 | async-start | bytes 4325376
  947.9 402.7 %reduce-scatter.23.cloned.1.call-start = ((), (), s32[]{:S(2)}) async-start(), calls=%async_computation.27 | async-start | bytes 4325376
  965.3 571.0 %reduce-scatter.15.cloned.1.call-start = ((), (), s32[]{:S(2)}) async-start(), calls=%async_computation.23 | async-start | bytes 17301504 | tf_op jit(solution)/shard_map/reduce_scatter | solution.py:348
  974.9 748.3 %reduce-scatter.17.cloned.1.call-start = ((), (), s32[]{:S(2)}) async-start(), calls=%async_computation.24 | async-start | bytes 17301504 | tf_op jit(solution)/shard_map/reduce_scatter | solution.py:350
  (56 other events, 1526.4 us)
Sparse Core Ops, SparseCore 0:
  10.9 57.6 all-gather.9
  71.5 55.6 all-gather.15
  130.0 55.3 all-gather.13
  187.3 49.6 all-gather.11
  239.0 49.2 all-gather.17
  291.0 54.9 all-gather.19
  348.8 76.4 all-gather.21
  428.1 76.0 all-gather.23
  530.8 163.3 reduce-scatter.12
  931.5 138.0 reduce-scatter.18
  1072.4 137.7 reduce-scatter.20
  1212.9 137.6 reduce-scatter.22
  1353.5 182.7 reduce-scatter.14
  1539.0 184.1 reduce-scatter.16
where the time goes:
time: 1740 us; the launch traced here: 1730 us
  waiting for transfers between devices  1240 us (71%)
  blocking collectives  158 us (9%)
  local copies, waits for them, and re-layouts  118 us (7%)
  matrix products  74 us (4%)
  loops' own time  54 us (3%)
  other arithmetic  37 us (2%)
  starting transfers between devices  34.3 us (2%)
    unnamed x17, waiting for transfers between devices  319 us
    ppermute x64, waiting for transfers between devices, passed_along(): return lax.ppermute(value, axis, pairs)  247 us
    reduce_scatter x1, waiting for transfers between devices, body(): lax.psum_scatter(grad_w2, ('head', 'blk'), scatter_dimension=0, tiled=True)  187 us
    reduce_scatter x1, waiting for transfers between devices, body(): lax.psum_scatter(grad_w1, ('head', 'blk'), scatter_dimension=0, tiled=True)  186 us
    unnamed x2, blocking collectives  81.3 us
    all_gather x1, waiting for transfers between devices, body(): lax.all_gather(w_inner, ('head', 'blk'), axis=0, tiled=True)  76.9 us
    all_gather x1, waiting for transfers between devices, body(): lax.all_gather(w_outer, ('head', 'blk'), axis=0, tiled=True)  69.3 us
    all_gather x1, waiting for transfers between devices, body(): lax.all_gather(w_key, ('head', 'blk'), axis=0, tiled=True)  59.1 us
  transfers between devices with their start and end apart: 81, of which 78 were waited for; matrix products, arithmetic and copies ran while one was open for 12% of the time, Pallas kernels for 0%

commit v1 on v0

--- a/solution.py
+++ b/solution.py
@@ -122,7 +122,12 @@
         lax.all_gather(gain_attn, ("head", "blk"), axis=0, tiled=True),
         lax.all_gather(shift_attn, ("head", "blk"), axis=0, tiled=True),
         lax.all_gather(w_inner, ("head", "blk"), axis=0, tiled=True),
-        lax.all_gather(b_inner, ("head", "blk"), axis=0, tiled=True),
+        jnp.concatenate(
+            lax.all_to_all(
+                jnp.stack([b_inner] * lax.axis_size(("head", "blk"))), ("head", "blk"), 0, 0
+            ),
+            axis=0,
+        ),
         lax.all_gather(w_outer, ("head", "blk"), axis=0, tiled=True),
         lax.all_gather(b_outer, ("head", "blk"), axis=0, tiled=True),
         lax.all_gather(gain_ffn, ("head", "blk"), axis=0, tiled=True),

time: 1740 us -> 1740 us (level)
  blocking collectives: 158 us -> 119 us
  waiting for transfers between devices: 1240 us -> 1270 us
    all_gather x1 -> x0, blocking collectives: 39.4 us -> none  [body(): lax.all_gather(b_inner, ('head', 'blk'), axis=0, tiled=True)]
    all_gather x1, waiting for transfers between devices: 3.66 us -> 38.3 us  [body(): key_piece = lax.all_gather(key_cols, 'blk', axis=0, tiled=True)]
  transfers between devices with their start and end apart: 81 -> 82, of which waited for: 78 -> 79; matrix products, arithmetic and copies ran while one was open for 12% -> 12% of each run, Pallas kernels for 0% -> 0%
where the time goes in v1:
time: 1740 us; the launch traced here: 1730 us
  waiting for transfers between devices  1270 us (73%)
  local copies, waits for them, and re-layouts  119 us (7%)
  blocking collectives  119 us (7%)
  matrix products  74 us (4%)
  loops' own time  54 us (3%)
  starting transfers between devices  40.9 us (2%)
  other arithmetic  37 us (2%)
    unnamed x17, waiting for transfers between devices  319 us
    ppermute x64, waiting for transfers between devices, passed_along(): return lax.ppermute(value, axis, pairs)  246 us
    reduce_scatter x1, waiting for transfers between devices, body(): lax.psum_scatter(grad_w2, ('head', 'blk'), scatter_dimension=0, tiled=True)  187 us
    reduce_scatter x1, waiting for transfers between devices, body(): lax.psum_scatter(grad_w1, ('head', 'blk'), scatter_dimension=0, tiled=True)  186 us
    unnamed x2, blocking collectives  81.5 us
    all_gather x1, waiting for transfers between devices, body(): lax.all_gather(w_inner, ('head', 'blk'), axis=0, tiled=True)  76.9 us
    all_gather x1, waiting for transfers between devices, body(): lax.all_gather(w_outer, ('head', 'blk'), axis=0, tiled=True)  69.3 us
    all_gather x1, waiting for transfers between devices, body(): lax.all_gather(w_key, ('head', 'blk'), axis=0, tiled=True)  59.1 us
  transfers between devices with their start and end apart: 82, of which 79 were waited for; matrix products, arithmetic and copies ran while one was open for 12% of the time, Pallas kernels for 0%

profile of v1, /device:TPU:4, one launch (start us, length us, event | category | flops | bytes accessed | tf_op | source)
XLA Modules:
  0.0 1729.0 jit_solution(9471488116752150321)
XLA Ops:
  9.5 59.1 %all-gather.9.cloned.1.call-done = bf16[1024,1024]{1,0:T(8,128)(2,1)} async-done(((bf16[32,1024]{1,0:T(8,128)(2,1)}), bf16[1024,1024]{1,0:T(8,128)(2,1)}) %all-gather.9.cloned.1.call-update) | async-done | bytes 2097168 | tf_op jit(solution)/shard_map/all_gather | solution.py:116
  70.8 7.8 all_to_all.152
  80.6 40.7 %all-reduce.18 = (bf16[1024]{0:T(1024)(128)(2,1)S(1)}, bf16[1024]{0:T(1024)(128)(2,1)S(1)}, bf16[1024]{0:T(1024)(128)(2,1)S(1)}, bf16[1024]{0:T(1024)(128)(2,1)S...) all-reduce(bf16[1024]{0:T(1024)(128)(2,1)S(1)} %dynamic-update-slic, ...), channel_id=1, replica_groups=mesh['head'=2,'blk'=16] {'head','blk'}, use_global_device_ids=true, to_apply=%add | all-reduce | flops 8192 | bytes 32768
  121.3 5.9 all-gather.15.cloned.1.call-done
  129.2 7.8 all_to_all.153
  139.7 4.9 all-to-all-start.4
  144.6 40.7 %all-gather.13.cloned.1.call-done = bf16[1024,1024]{1,0:T(8,128)(2,1)} async-done(((bf16[32,1024]{1,0:T(8,128)(2,1)}), bf16[1024,1024]{1,0:T(8,128)(2,1)}) %all-gather.13.cloned.1.call-update) | async-done | bytes 2097168 | tf_op jit(solution)/shard_map/all_gather | solution.py:115
  188.1 4.5 all-to-all-start.1
  192.8 4.0 all-to-all-done.1
  198.5 38.3 %all-gather.11.cloned.1.call-done = bf16[4096,512]{1,0:T(8,128)(2,1)} async-done(((bf16[256,512]{1,0:T(8,128)(2,1)}), bf16[4096,512]{1,0:T(8,128)(2,1)}) %all-gather.11.cloned.1.call-update) | async-done | bytes 4194320 | tf_op jit(solution)/shard_map/all_gather | solution.py:181
  236.8 11.3 reshape.276
  248.1 9.9 copy.106
  258.0 30.1 %all-gather.17.cloned.1.call-done = bf16[4096,512]{1,0:T(8,128)(2,1)} async-done(((bf16[256,512]{1,0:T(8,128)(2,1)}), bf16[4096,512]{1,0:T(8,128)(2,1)}) %all-gather.17.cloned.1.call-update) | async-done | bytes 4194320 | tf_op jit(solution)/shard_map/all_gather | solution.py:182
  288.1 11.2 reshape.277
  299.3 9.8 copy.107
  309.1 23.4 %while.38 = (s32[]{:T(128)}, f32[8,256]{1,0:T(8,128)S(1)}, f32[8,256]{1,0:T(8,128)S(1)}, f32[8,256,64]{1,2,0:T(8,128)S(1)}, s32[4,1024]{1,0:T(4,128)S(1)}, /*ind...) while((s32[]{:T(128)}, f32[8,256]{1,0:T(8,128)S(1)}, ...), condition=%wide.region_5.6_spmd, body=%wide.region_0.5_spmd.sunk | while | flops 560467968 | bytes 29768016 | solution.py:206
  312.9 8.1 conditional.5
  317.7 3.3 fusion.6
  333.5 4.1 all-to-all-start.3
  337.6 8.2 all-gather.19.cloned.1.call-done
  348.2 76.9 %all-gather.21.cloned.1.call-done = bf16[1024,4096]{1,0:T(8,128)(2,1)} async-done(((bf16[32,4096]{1,0:T(8,128)(2,1)}), bf16[1024,4096]{1,0:T(8,128)(2,1)}) %all-gather.21.cloned.1.call-update) | async-done | bytes 8388624 | tf_op jit(solution)/shard_map/all_gather | solution.py:124
  425.1 9.6 multiply_convert_fusion.1
  434.7 69.3 %all-gather.23.cloned.1.call-done = bf16[4096,1024]{1,0:T(8,128)(2,1)} async-done(((bf16[128,1024]{1,0:T(8,128)(2,1)}), bf16[4096,1024]{1,0:T(8,128)(2,1)}) %all-gather.23.cloned.1.call-update) | async-done | bytes 8388624 | tf_op jit(solution)/shard_map/all_gather | solution.py:131
  504.0 5.3 fusion.53
  511.1 5.3 convert_reduce_fusion
  516.5 3.1 multiply_reduce_fusion
  522.9 4.0 all-to-all-start.5
  531.5 384.1 %while.39 = (s32[]{:T(128)}, bf16[256,8,64]{0,2,1:T(8,128)(2,1)}, bf16[256,8,64]{0,2,1:T(8,128)(2,1)S(1)}, f32[256,8,64]{0,2,1:T(8,128)S(1)}, f32[256,8,64]{0,2,...) while((s32[]{:T(128)}, bf16[256,8,64]{0,2,1:T(8,128)(2,1)}, ...), condition=%wide.region_18.19_spmd.clone, body=%wide.region_15.18_spmd.clone.sunk | while | flops 340721696 | bytes 25055948 | solution.py:303
  542.6 5.2 collective-permute-done.2
  547.8 3.7 collective-permute-done.3
  568.7 4.4 collective-permute-done.2
  579.5 3.2 collective-permute-done.1
  591.9 5.9 collective-permute-done.2
  601.6 3.1 collective-permute-done
  614.8 8.2 collective-permute-done.2
  623.1 3.2 collective-permute-done.3
  639.4 8.9 collective-permute-done.2
  655.0 3.1 collective-permute-done.1
  664.4 8.5 collective-permute-done.2
  673.0 3.3 collective-permute-done.3
  689.1 8.2 collective-permute-done.2
  712.2 8.2 collective-permute-done.2
  735.2 8.2 collective-permute-done.2
  758.2 8.2 collective-permute-done.2
  781.2 8.2 collective-permute-done.2
  804.5 8.0 collective-permute-done.2
  828.4 7.1 collective-permute-done.2
  852.3 6.2 collective-permute-done.2
  876.2 5.4 collective-permute-done.2
  900.0 7.1 collective-permute-done.2
  915.8 6.3 all_to_all.154
  925.5 5.4 copy.128
  931.1 7.6 all_to_all.155
  942.0 5.4 copy.130
  948.6 8.1 all_to_all.156
  959.4 5.4 copy.132
  966.2 8.2 fusion.42
  975.7 8.1 fusion.55
  985.1 40.8 %all-reduce.17 = (f32[1024]{0:T(1024)S(1)}, f32[1024]{0:T(1024)S(1)}, f32[1024]{0:T(1024)S(1)}, f32[1024]{0:T(1024)S(1)}, f32[1024]{0:T(1024)S(1)}, /*index=5*/f...) all-reduce(f32[1024]{0:T(1024)S(1)} %bitcast.193, ...), channel_id=5, replica_groups=mesh['head'=2,'blk'=16] {'head','blk'}, use_global_device_ids=true, to_apply=%region_23.24.clone | all-reduce | flops 12288 | bytes 98304
  1035.3 33.7 %reduce-scatter.19.cloned.1.call-done = f32[32,1024]{1,0:T(8,128)} async-done(((f32[1024,1024]{1,0:T(8,128)}), f32[32,1024]{1,0:T(8,128)}) %reduce-scatter.19.cloned.1.call-update) | async-done | bytes 131088
  1069.0 140.6 %reduce-scatter.21.cloned.1.call-done = f32[32,1024]{1,0:T(8,128)} async-done(((f32[1024,1024]{1,0:T(8,128)}), f32[32,1024]{1,0:T(8,128)}) %reduce-scatter.21.cloned.1.call-update) | async-done | bytes 131088
  1209.5 140.1 %reduce-scatter.23.cloned.1.call-done = f32[32,1024]{1,0:T(8,128)} async-done(((f32[1024,1024]{1,0:T(8,128)}), f32[32,1024]{1,0:T(8,128)}) %reduce-scatter.23.cloned.1.call-update) | async-done | bytes 131088
  1349.7 185.6 %reduce-scatter.15.cloned.1.call-done = f32[32,4096]{1,0:T(8,128)} async-done(((f32[1024,4096]{1,0:T(8,128)}), f32[32,4096]{1,0:T(8,128)}) %reduce-scatter.15.cloned.1.call-update) | async-done | bytes 524304 | tf_op jit(solution)/shard_map/reduce_scatter | solution.py:353
  1535.3 187.0 %reduce-scatter.17.cloned.1.call-done = f32[128,1024]{1,0:T(8,128)} async-done(((f32[4096,1024]{1,0:T(8,128)}), f32[128,1024]{1,0:T(8,128)}) %reduce-scatter.17.cloned.1.call-update) | async-done | bytes 524304 | tf_op jit(solution)/shard_map/reduce_scatter | solution.py:355
  (527 shorter events, 272.8 us)
Async XLA Ops:
  7.3 61.4 %all-gather.9.cloned.1.call-start = ((), (), s32[]{:S(2)}) async-start(), calls=%async_computation.15 | async-start | bytes 2162688 | tf_op jit(solution)/shard_map/all_gather | solution.py:116
  8.0 119.1 %all-gather.15.cloned.1.call-start = ((), (), s32[]{:S(2)}) async-start(), calls=%async_computation.18 | async-start | bytes 2162688 | tf_op jit(solution)/shard_map/all_gather | solution.py:117
  8.8 176.6 %all-gather.13.cloned.1.call-start = ((), (), s32[]{:S(2)}) async-start(), calls=%async_computation.17 | async-start | bytes 2162688 | tf_op jit(solution)/shard_map/all_gather | solution.py:115
  9.5 227.3 %all-gather.11.cloned.1.call-start = ((), (), s32[]{:S(2)}) async-start(), calls=%async_computation.16 | async-start | bytes 4456448 | tf_op jit(solution)/shard_map/all_gather | solution.py:181
  78.6 209.5 %all-gather.17.cloned.1.call-start = ((), (), s32[]{:S(2)}) async-start(), calls=%async_computation.19 | async-start | bytes 4456448 | tf_op jit(solution)/shard_map/all_gather | solution.py:182
  137.0 208.8 %all-gather.19.cloned.1.call-start = ((), (), s32[]{:S(2)}) async-start(), calls=%async_computation.20 | async-start | bytes 2162688 | tf_op jit(solution)/shard_map/all_gather | solution.py:120
  137.6 287.5 %all-gather.21.cloned.1.call-start = ((), (), s32[]{:S(2)}) async-start(), calls=%async_computation.21 | async-start | bytes 8650752 | tf_op jit(solution)/shard_map/all_gather | solution.py:124
  138.4 365.7 %all-gather.23.cloned.1.call-start = ((), (), s32[]{:S(2)}) async-start(), calls=%async_computation.22 | async-start | bytes 8650752 | tf_op jit(solution)/shard_map/all_gather | solution.py:131
  139.7 48.4 %all-to-all-start.4 = ((bf16[32,1,128]{2,1,0:T(2,128)(2,1)}), bf16[32,1,128]{2,1,0:T(2,128)(2,1)S(1)}, u32[]{:S(2)}, u32[]{:S(2)}) async-start(bf16[32,1,128]{2,1,0:T(2,128)(2,1)} %stack.2), calls=%async_computation.4 | async-start | bytes 32768 | tf_op jit(solution)/shard_map/all_to_all | solution.py:126
  333.5 12.3 all-to-all-start.3
  526.9 508.4 %reduce-scatter.13.cloned.1.call-start = ((), (), s32[]{:S(2)}) async-start(), calls=%async_computation.23 | async-start | bytes 4325376 | tf_op jit(solution)/shard_map/reduce_scatter | solution.py:349
  529.9 539.1 %reduce-scatter.19.cloned.1.call-start = ((), (), s32[]{:S(2)}) async-start(), calls=%async_computation.26 | async-start | bytes 4325376
  539.3 12.2 collective-permute-start.3
  540.9 14.1 collective-permute-start
  541.0 16.7 collective-permute-start.1
  564.3 11.7 collective-permute-start.3
  566.9 12.6 collective-permute-start
  566.9 15.8 collective-permute-start.1
  588.9 11.9 collective-permute-start.3
  589.7 15.0 collective-permute-start
  589.8 18.0 %collective-permute-start.1 = (bf16[256,8,64]{0,2,1:T(8,128)(2,1)S(1)}, bf16[256,8,64]{0,2,1:T(8,128)(2,1)S(1)}, u32[]{:S(2)}, u32[]{:S(2)}) collective-permute-start(bf16[256,8,64]{0,2,1:T(8,128)(2,1)S(1)} %copy.190), channel_id=1, source_target_pairs={{0,1},{1,2},{2,3},{3,4},{4,5},{5,6},{6,7},{7,8},{8,9},{9,10},{10,1... | collective-permute-start | bytes 786440 | tf_op jit(solution)/shard_map/while/body/eval_jaxpr/ppermute | solution.py:16
  613.9 12.3 collective-permute-start.3
  614.0 16.1 collective-permute-start
  614.1 18.9 %collective-permute-start.1 = (bf16[256,8,64]{0,2,1:T(8,128)(2,1)S(1)}, bf16[256,8,64]{0,2,1:T(8,128)(2,1)S(1)}, u32[]{:S(2)}, u32[]{:S(2)}) collective-permute-start(bf16[256,8,64]{0,2,1:T(8,128)(2,1)S(1)} %copy.190), channel_id=1, source_target_pairs={{0,1},{1,2},{2,3},{3,4},{4,5},{5,6},{6,7},{7,8},{8,9},{9,10},{10,1... | collective-permute-start | bytes 786440 | tf_op jit(solution)/shard_map/while/body/eval_jaxpr/ppermute | solution.py:16
  639.2 11.9 collective-permute-start.3
  639.2 15.8 collective-permute-start
  639.3 18.8 %collective-permute-start.1 = (bf16[256,8,64]{0,2,1:T(8,128)(2,1)S(1)}, bf16[256,8,64]{0,2,1:T(8,128)(2,1)S(1)}, u32[]{:S(2)}, u32[]{:S(2)}) collective-permute-start(bf16[256,8,64]{0,2,1:T(8,128)(2,1)S(1)} %copy.190), channel_id=1, source_target_pairs={{0,1},{1,2},{2,3},{3,4},{4,5},{5,6},{6,7},{7,8},{8,9},{9,10},{10,1... | collective-permute-start | bytes 786440 | tf_op jit(solution)/shard_map/while/body/eval_jaxpr/ppermute | solution.py:16
  664.2 12.0 collective-permute-start.3
  664.3 15.6 collective-permute-start
  664.4 18.4 %collective-permute-start.1 = (bf16[256,8,64]{0,2,1:T(8,128)(2,1)S(1)}, bf16[256,8,64]{0,2,1:T(8,128)(2,1)S(1)}, u32[]{:S(2)}, u32[]{:S(2)}) collective-permute-start(bf16[256,8,64]{0,2,1:T(8,128)(2,1)S(1)} %copy.190), channel_id=1, source_target_pairs={{0,1},{1,2},{2,3},{3,4},{4,5},{5,6},{6,7},{7,8},{8,9},{9,10},{10,1... | collective-permute-start | bytes 786440 | tf_op jit(solution)/shard_map/while/body/eval_jaxpr/ppermute | solution.py:16
  688.9 11.3 collective-permute-start.3
  689.0 14.1 collective-permute-start
  689.1 16.7 collective-permute-start.1
  712.0 11.3 collective-permute-start.3
  712.0 14.1 collective-permute-start
  712.1 16.7 collective-permute-start.1
  735.0 11.3 collective-permute-start.3
  735.0 14.1 collective-permute-start
  735.1 16.7 collective-permute-start.1
  758.0 11.3 collective-permute-start.3
  758.1 14.1 collective-permute-start
  758.1 16.7 collective-permute-start.1
  781.0 11.3 collective-permute-start.3
  781.1 14.1 collective-permute-start
  781.1 16.7 collective-permute-start.1
  804.0 11.3 collective-permute-start.3
  804.1 14.1 collective-permute-start
  804.1 16.7 collective-permute-start.1
  827.0 11.3 collective-permute-start.3
  827.1 14.1 collective-permute-start
  827.2 16.7 collective-permute-start.1
  850.0 11.3 collective-permute-start.3
  850.1 14.1 collective-permute-start
  850.2 16.7 collective-permute-start.1
  873.1 11.3 collective-permute-start.3
  873.1 14.1 collective-permute-start
  873.2 16.7 collective-permute-start.1
  898.7 11.3 collective-permute-start.3
  898.8 14.1 collective-permute-start
  898.9 16.7 collective-permute-start.1
  930.9 278.6 %reduce-scatter.21.cloned.1.call-start = ((), (), s32[]{:S(2)}) async-start(), calls=%async_computation.27 | async-start | bytes 4325376
  947.5 402.2 %reduce-scatter.23.cloned.1.call-start = ((), (), s32[]{:S(2)}) async-start(), calls=%async_computation.28 | async-start | bytes 4325376
  964.8 570.4 %reduce-scatter.15.cloned.1.call-start = ((), (), s32[]{:S(2)}) async-start(), calls=%async_computation.24 | async-start | bytes 17301504 | tf_op jit(solution)/shard_map/reduce_scatter | solution.py:353
  974.4 747.8 %reduce-scatter.17.cloned.1.call-start = ((), (), s32[]{:S(2)}) async-start(), calls=%async_computation.25 | async-start | bytes 17301504 | tf_op jit(solution)/shard_map/reduce_scatter | solution.py:355
  (57 other events, 1384.8 us)
Sparse Core Ops, SparseCore 0:
  10.9 57.6 all-gather.8
  71.5 55.6 all-gather.14
  130.0 55.3 all-gather.12
  187.4 49.4 all-gather.10
  238.8 49.2 all-gather.16
  290.8 54.9 all-gather.18
  348.6 76.4 all-gather.20
  427.9 76.0 all-gather.22
  530.6 162.5 reduce-scatter.12
  931.0 137.9 reduce-scatter.18
  1071.8 137.6 reduce-scatter.20
  1212.2 137.3 reduce-scatter.22
  1352.5 182.6 reduce-scatter.14
  1538.0 184.1 reduce-scatter.16
